TPU v7x, 256 devices: a whole 4x4x8 slice. The times are simulated.
256 devices in a mesh: grp: 8 (over z), tp: 32 (over x, y, core).
Axes of the slice: x: 4, y: 4, z: 8, core: 2. Of those that a mesh axis runs over, the one named last changes fastest.
Arguments:
- hidden: bfloat16 [8192, 20480], P('grp', 'tp'), may hold values from -6 to 6
- down_weight: bfloat16 [20480, 8192], P('tp'), may hold values from -0.078125 to 0.078125
- adapter_down_factor: bfloat16 [64, 64, 20480], P('grp', None, 'tp'), may hold values from -0.0390625 to 0.0390625
- adapter_up_factor: bfloat16 [64, 64, 8192], P('grp', None, 'tp'), may hold values from -0.75 to 0.75
- row_tile_adapter: int32 [64], P('grp'), may hold values from 0 to 63, as said below
- adapter_pool_slot: int32 [64], replicated, may hold values from 0 to 63, as said below
Outputs:
- output: bfloat16 [8192, 8192], P('grp', 'tp')
Inputs may be any that keep to these rules, and one draw needn't show every extreme that they name: adapter_pool_slot is a permutation; slot s of the pool is held by group s // 8. `row_tile_adapter`: at most 4 tiles of one group have adapters held by one owner group, and in every draw one owner group holds the adapters of exactly 4 tiles of every group.
All inputs are finite; a program needn't handle non-finite values.
Results may differ from a plain program's by a relative error of at most 0.019.
Values may be sent and summed in bfloat16 or wider, within the bound.
A program may use at most 128 MiB of HBM per device.

v0:
```python
import jax
import jax.numpy as jnp
from jax import lax
from jax.sharding import PartitionSpec as P

adapter_scale = 2.0


def local(
    hidden, down_weight, adapter_down_factor, adapter_up_factor, row_tile_adapter, adapter_pool_slot
):
    tok_rows, feat_cols = hidden.shape
    tile_count = row_tile_adapter.shape[0]
    tile_rows = tok_rows // tile_count
    slot_table = adapter_pool_slot[row_tile_adapter]
    base_cols = lax.psum_scatter(
        lax.dot_general(
            down_weight, hidden, (((0,), (1,)), ((), ())), preferred_element_type=jnp.float32
        ).astype(jnp.bfloat16),
        "tp",
        scatter_dimension=0,
        tiled=True,
    ).astype(jnp.float32)
    pooled_down, pooled_up = (
        lax.all_gather(adapter_down_factor, "grp", axis=0, tiled=True),
        lax.all_gather(adapter_up_factor, "grp", axis=0, tiled=True),
    )
    tile_blocks = hidden.reshape(tile_count, tile_rows, feat_cols)
    rank_part = jnp.einsum(
        "ktf,krf->ktr", tile_blocks, pooled_down[slot_table], preferred_element_type=jnp.float32
    )
    rank_projections = lax.psum(rank_part.astype(jnp.bfloat16), "tp")
    adapted_output = (
        jnp.einsum(
            "pjf,pfb->pjb",
            rank_projections,
            pooled_up[slot_table],
            preferred_element_type=jnp.float32,
        )
        * adapter_scale
    ).astype(jnp.bfloat16)
    adapter_delta = adapted_output.reshape(tok_rows, -1).astype(jnp.float32)
    return (base_cols.T + adapter_delta).astype(jnp.bfloat16)


def solution(mesh):
    placed = (
        P("grp", "tp"),
        P("tp", None),
        P("grp", None, "tp"),
        P("grp", None, "tp"),
        P("grp"),
        P(),
    )
    return jax.shard_map(
        local, mesh=mesh, in_specs=placed, out_specs=P("grp", "tp"), check_vma=False
    )
```

profile of v0, /device:TPU:2, one launch (start us, length us, event | category | flops | bytes accessed | tf_op | source)
XLA Modules:
  0.0 366.4 jit_solution(15145106554480718428)
XLA Ops:
  6.5 0.0 copy-start
  6.5 0.0 all-gather.3.cloned.1.call-start
  6.5 0.7 all-gather.3.cloned.1.call-update
  7.3 0.0 all-gather.5.cloned.1.call-start
  7.3 0.7 all-gather.5.cloned.1.call-update
  8.0 0.0 all-reduce.2.cloned.1.call-start
  8.1 0.7 compare_select_fusion.1
  8.7 1.3 gather_fusion
  10.0 66.6 %all-gather.3.cloned.1.call-done = bf16[64,64,640]{2,1,0:T(8,128)(2,1)} async-done(((bf16[8,64,640]{2,1,0:T(8,128)(2,1)}), bf16[64,64,640]{2,1,0:T(8,128)(2,1)}) %all-gather.3.cloned.1.call-update) | async-done | bytes 5242896 | tf_op jit(solution)/shard_map/all_gather | solution.py:25
  76.7 3.1 gather_fusion.1
  79.9 1.3 fusion.1
  81.1 0.0 all-reduce.2.cloned.1.call-update
  81.2 0.0 reduce-scatter.2.cloned.1.call-start
  81.2 20.1 %convolution_convert_fusion = bf16[8192,1024]{1,0:T(8,128)(2,1)} fusion(bf16[640,8192]{1,0:T(8,128)(2,1)} %param.7, bf16[1024,640]{1,0:T(8,128)(2,1)S(1)} %copy-done), kind=kOutput, calls=%fused_computation.3 | convolution fusion | flops 10745806848 | bytes 28573696 | tf_op jit(solution)/shard_map/dot_general | solution.py:17
  101.3 0.0 reduce-scatter.2.cloned.1.call-update
  101.3 16.6 %all-gather.5.cloned.1.call-done = bf16[64,64,256]{2,1,0:T(8,128)(2,1)} async-done(((bf16[8,64,256]{2,1,0:T(8,128)(2,1)}), bf16[64,64,256]{2,1,0:T(8,128)(2,1)}) %all-gather.5.cloned.1.call-update) | async-done | bytes 2097168 | tf_op jit(solution)/shard_map/all_gather | solution.py:26
  118.0 2.2 gather_fusion.2
  120.1 110.5 %all-reduce.2.cloned.1.call-done = bf16[8,128,64]{1,2,0:T(8,128)(2,1)} async-done(((bf16[8,128,64]{1,2,0:T(8,128)(2,1)}), bf16[8,128,64]{1,2,0:T(8,128)(2,1)}) %all-reduce.2.cloned.1.call-update) | async-done | bytes 131088 | tf_op jit(solution)/shard_map/psum | solution.py:32
  230.6 1.2 fusion
  231.8 0.1 bitcast_convert_fusion
  231.9 0.3 copy.13
  232.3 125.4 %reduce-scatter.2.cloned.1.call-done = bf16[256,1024]{1,0:T(8,128)(2,1)} async-done(((bf16[8192,1024]{1,0:T(8,128)(2,1)}), bf16[256,1024]{1,0:T(8,128)(2,1)}) %reduce-scatter.2.cloned.1.call-update) | async-done | bytes 524304 | tf_op jit(solution)/shard_map/reduce_scatter | solution.py:16
  357.7 1.2 fusion.2
  358.9 1.0 copy.12
  (4 shorter events, 0.0 us)
Async XLA Ops:
  6.5 73.3 %copy-start = (bf16[1024,640]{1,0:T(8,128)(2,1)S(1)}, bf16[1024,640]{1,0:T(8,128)(2,1)}, u32[]{:S(2)}) copy-start(bf16[1024,640]{1,0:T(8,128)(2,1)} %param.6) | copy-start | bytes 3932164
  6.5 70.1 %all-gather.3.cloned.1.call-start = ((), (), s32[]{:S(2)}) async-start(), calls=%async_computation.2 | async-start | bytes 5898240 | tf_op jit(solution)/shard_map/all_gather | solution.py:25
  7.3 110.7 %all-gather.5.cloned.1.call-start = ((), (), s32[]{:S(2)}) async-start(), calls=%async_computation.4 | async-start | bytes 2359296 | tf_op jit(solution)/shard_map/all_gather | solution.py:26
  8.0 222.6 %all-reduce.2.cloned.1.call-start = ((), (), s32[]{:S(2)}) async-start(), calls=%async_computation.3 | async-start | bytes 262144 | tf_op jit(solution)/shard_map/psum | solution.py:32
  81.2 276.6 %reduce-scatter.2.cloned.1.call-start = ((), (), s32[]{:S(2)}) async-start(), calls=%async_computation.1 | async-start | bytes 17301504 | tf_op jit(solution)/shard_map/reduce_scatter | solution.py:16
Sparse Core Ops, SparseCore 0:
  9.1 67.5 all-gather.2
  78.5 39.4 all-gather.4
  121.2 109.3 all-reduce.1
  234.6 123.0 reduce-scatter.1
where the time goes:
time: 367 us; the launch traced here: 366 us
  waiting for transfers between devices  321 us (87%)
  matrix products  22.6 us (6%)
  between operations  13.2 us (4%)
  local copies, waits for them, and re-layouts  7.93 us (2%)
    reduce_scatter x1, waiting for transfers between devices, local(): lax.psum_scatter(lax.dot_general(down_weight, hidden, (((0,), (1,)), ((),...  125 us
    psum x1, waiting for transfers between devices, local(): rank_projections = lax.psum(rank_part.astype(jnp.bfloat16), 'tp')  110 us
    all_gather x1, waiting for transfers between devices, local(): lax.all_gather(adapter_down_factor, 'grp', axis=0, tiled=True)  66.6 us
    dot_general x1, matrix products, local(): lax.dot_general(down_weight, hidden, (((0,), (1,)), ((), ())), preferred_...  20.1 us
    all_gather x1, waiting for transfers between devices, local(): lax.all_gather(adapter_up_factor, 'grp', axis=0, tiled=True)  16.6 us
  transfers between devices with their start and end apart: 4, of which 4 were waited for; matrix products, arithmetic and copies ran while one was open for 8% of the time, Pallas kernels for 0%

commit v1 on v0

--- a/solution.py
+++ b/solution.py
@@ -29,7 +29,7 @@
     rank_part = jnp.einsum(
         "ktf,krf->ktr", tile_blocks, pooled_down[slot_table], preferred_element_type=jnp.float32
     )
-    rank_projections = lax.psum(rank_part.astype(jnp.bfloat16), "tp")
+    rank_projections = jnp.sum(lax.all_gather(rank_part.astype(jnp.bfloat16), "tp"), axis=0)
     adapted_output = (
         jnp.einsum(
             "pjf,pfb->pjb",

time: 367 us -> 305 us (0.83)
  waiting for transfers between devices: 321 us -> 257 us
    psum x1 -> x0, waiting for transfers between devices: 110 us -> none  [local(): rank_projections = lax.psum(rank_part.astype(jnp.bfloat16), 'tp')]
    all_gather x0 -> x1, waiting for transfers between devices: none -> 49.7 us  [local(): lax.all_gather(rank_part.astype(jnp.bfloat16), 'tp')]
  transfers between devices with their start and end apart: 4 -> 4, of which waited for: 4 -> 4; matrix products, arithmetic and copies ran while one was open for 8% -> 11% of each run, Pallas kernels for 0% -> 0%
where the time goes in v1:
time: 305 us
  waiting for transfers between devices  257 us (84%)
  matrix products  21.7 us (7%)
  between operations  13.2 us (4%)
  local copies, waits for them, and re-layouts  7.93 us (3%)
  other arithmetic  5.1 us (2%)
    reduce_scatter x1, waiting for transfers between devices, local(): lax.psum_scatter(lax.dot_general(down_weight, hidden, (((0,), (1,)), ((),...  123 us
    all_gather x1, waiting for transfers between devices, local(): lax.all_gather(adapter_down_factor, 'grp', axis=0, tiled=True)  66.6 us
    all_gather x1, waiting for transfers between devices, local(): lax.all_gather(rank_part.astype(jnp.bfloat16), 'tp')  49.7 us
    dot_general x1, matrix products, local(): lax.dot_general(down_weight, hidden, (((0,), (1,)), ((), ())), preferred_...  20.1 us
    all_gather x1, waiting for transfers between devices, local(): lax.all_gather(adapter_up_factor, 'grp', axis=0, tiled=True)  16.6 us
  transfers between devices with their start and end apart: 4, of which 4 were waited for; matrix products, arithmetic and copies ran while one was open for 11% of the time, Pallas kernels for 0%

profile of v1, /device:TPU:2, one launch (start us, length us, event | category | flops | bytes accessed | tf_op | source)
XLA Modules:
  0.0 305.1 jit_solution(18378733527413806491)
XLA Ops:
  6.5 0.0 copy-start
  6.5 0.7 all-gather.5.cloned.1.call-update
  7.3 0.0 all-gather.7.cloned.1.call-start
  7.3 0.7 all-gather.7.cloned.1.call-update
  8.0 0.0 all-gather.9.cloned.1.call-start
  8.1 0.7 compare_select_fusion.1
  8.7 1.3 gather_fusion
  10.0 66.6 %all-gather.5.cloned.1.call-done = bf16[64,64,640]{2,1,0:T(8,128)(2,1)} async-done(((bf16[8,64,640]{2,1,0:T(8,128)(2,1)}), bf16[64,64,640]{2,1,0:T(8,128)(2,1)}) %all-gather.5.cloned.1.call-update) | async-done | bytes 5242896 | tf_op jit(solution)/shard_map/all_gather | solution.py:25
  76.7 3.1 %gather_fusion.1 = bf16[8,64,640]{2,1,0:T(8,128)(2,1)S(1)} fusion(bf16[64,64,640]{2,1,0:T(8,128)(2,1)} %all-gather.5.cloned.1.call-done, s32[1024]{0:T(1024)S(1)} %pad_clamp_fusion), kind=kCustom, calls=%fused_computation.1 | custom fusion | bytes 1310752 | tf_op jit(solution)/shard_map/gather | solution.py:30
  79.9 1.3 fusion.1
  81.1 0.0 all-gather.9.cloned.1.call-update
  81.2 0.0 reduce-scatter.2.cloned.1.call-start
  81.2 20.1 %convolution_convert_fusion = bf16[8192,1024]{1,0:T(8,128)(2,1)} fusion(bf16[640,8192]{1,0:T(8,128)(2,1)} %param.7, bf16[1024,640]{1,0:T(8,128)(2,1)S(1)} %copy-done), kind=kOutput, calls=%fused_computation.3 | convolution fusion | flops 10745806848 | bytes 28573696 | tf_op jit(solution)/shard_map/dot_general | solution.py:17
  101.3 0.0 reduce-scatter.2.cloned.1.call-update
  101.3 16.6 %all-gather.7.cloned.1.call-done = bf16[64,64,256]{2,1,0:T(8,128)(2,1)} async-done(((bf16[8,64,256]{2,1,0:T(8,128)(2,1)}), bf16[64,64,256]{2,1,0:T(8,128)(2,1)}) %all-gather.7.cloned.1.call-update) | async-done | bytes 2097168 | tf_op jit(solution)/shard_map/all_gather | solution.py:26
  118.0 2.2 gather_fusion.2
  120.1 49.7 %all-gather.9.cloned.1.call-done = bf16[256,128,64]{1,2,0:T(8,128)(2,1)} async-done(((bf16[8,128,64]{1,2,0:T(8,128)(2,1)}), bf16[256,128,64]{1,2,0:T(8,128)(2,1)}) %all-gather.9.cloned.1.call-update) | async-done | bytes 4194320 | tf_op jit(solution)/shard_map/all_gather | solution.py:32
  169.9 3.1 %reduce_sum.12 = bf16[8,128,64]{1,2,0:T(8,128)(2,1)S(1)} reduce(bf16[32,8,128,64]{2,3,1,0:T(8,128)(2,1)} %bitcast.22, bf16[]{:T(256)} %constant.3.clone.1), dimensions={0}, to_apply=%region_1.0 | reduce | flops 2031616 | bytes 4325378 | tf_op jit(solution)/shard_map/reduce_sum | solution.py:32
  173.0 0.3 fusion
  173.3 0.1 bitcast_convert_fusion
  173.5 0.3 copy.13
  173.8 122.6 %reduce-scatter.2.cloned.1.call-done = bf16[256,1024]{1,0:T(8,128)(2,1)} async-done(((bf16[8192,1024]{1,0:T(8,128)(2,1)}), bf16[256,1024]{1,0:T(8,128)(2,1)}) %reduce-scatter.2.cloned.1.call-update) | async-done | bytes 524304 | tf_op jit(solution)/shard_map/reduce_scatter | solution.py:16
  296.4 1.2 fusion.2
  297.6 1.0 copy.12
  (5 shorter events, 0.0 us)
Async XLA Ops:
  6.5 73.3 %copy-start = (bf16[1024,640]{1,0:T(8,128)(2,1)S(1)}, bf16[1024,640]{1,0:T(8,128)(2,1)}, u32[]{:S(2)}) copy-start(bf16[1024,640]{1,0:T(8,128)(2,1)} %param.6) | copy-start | bytes 3932164
  6.5 70.1 %all-gather.5.cloned.1.call-start = ((), (), s32[]{:S(2)}) async-start(), calls=%async_computation.2 | async-start | bytes 5898240 | tf_op jit(solution)/shard_map/all_gather | solution.py:25
  7.3 110.7 %all-gather.7.cloned.1.call-start = ((), (), s32[]{:S(2)}) async-start(), calls=%async_computation.3 | async-start | bytes 2359296 | tf_op jit(solution)/shard_map/all_gather | solution.py:26
  8.0 161.8 %all-gather.9.cloned.1.call-start = ((), (), s32[]{:S(2)}) async-start(), calls=%async_computation.4 | async-start | bytes 4325376 | tf_op jit(solution)/shard_map/all_gather | solution.py:32
  81.2 215.2 %reduce-scatter.2.cloned.1.call-start = ((), (), s32[]{:S(2)}) async-start(), calls=%async_computation.1 | async-start | bytes 17301504 | tf_op jit(solution)/shard_map/reduce_scatter | solution.py:16
Sparse Core Ops, SparseCore 0:
  9.1 67.5 all-gather.4
  78.5 39.4 all-gather.6
  120.5 49.2 all-gather.8
  173.9 122.4 reduce-scatter.1
